TPU v7x, 256 devices: a whole 4x4x8 slice. The times are simulated.
256 devices in a mesh: row: 8 (over z_hi, core), col: 32 (over x, z_lo, y).
Axes of the slice: x: 4, y: 4, z: 8 (z_hi: 4, z_lo: 2; z = z_hi * 2 + z_lo), core: 2. Of those that a mesh axis runs over, the one named last changes fastest.
Arguments:
- basis_out: float32 [16384, 16384], P('row', 'col'), may hold values from -0.046875 to 0.046875
- basis_in: float32 [16384, 16384], P('col', 'row'), may hold values from -0.046875 to 0.046875
- eig_damped: float32 [16384, 16384], P('col', 'row'), may hold values from 0.5 to 8
- query_left: bfloat16 [16384, 256], P(('row', 'col')), may hold values from -0.375 to 0.375
- query_right: bfloat16 [16384, 256], P('col'), may hold values from -6 to 6
- train_left: bfloat16 [16384, 512], P(('row', 'col')), may hold values from -0.046875 to 0.046875
- train_right: bfloat16 [16384, 512], P('col'), may hold values from -0.046875 to 0.046875
Outputs:
- response: float32 [16384, 512], P(('row', 'col'))
- scores: float32 [512], replicated
All inputs are finite; a program needn't handle non-finite values.
Results may differ from a plain program's by a relative error of at most 0.0003.
Values may be sent and summed in bfloat16 or wider, within the bound.
No kernel may reach another device: no remote copies, remote signals or barrier semaphores. Data moves between devices by JAX's collectives and lax.ppermute only.
A program may use at most 128 MiB of HBM per device.

v0:
```python
import jax
import jax.numpy as jnp
from jax import lax
from jax.sharding import Mesh
from jax.sharding import PartitionSpec as P

COL = ("col_0", "col_1", "col_2")
ROW = ("row_0", "row_1")
ROW_COL = ("row_0", "row_1", "col_0", "col_1", "col_2")


def joined_along(pieces, dim):
    dims = list(pieces.shape[1:])
    dims[dim] *= pieces.shape[0]
    return jnp.moveaxis(pieces, 0, dim).reshape(dims)


def from_everyone(array, axis):
    copies = jnp.broadcast_to(array, (lax.axis_size(axis), *array.shape))
    return lax.all_to_all(copies, axis, split_axis=0, concat_axis=0, tiled=True)


def gathered_copies(array, axis, dim):
    return joined_along(from_everyone(array, axis), dim)


def over_copies(array, axis):
    everything = from_everyone(array, axis)
    return jnp.sum(everything, axis=0)


def sum_in_order(pieces, axes, turns):
    dims = [lax.axis_size(a) for a in axes]
    pieces = pieces.reshape(*dims, *pieces.shape[1:])
    pieces = pieces.transpose(*turns, *range(len(axes), pieces.ndim))
    pieces = pieces.reshape(-1, *pieces.shape[len(axes) :])
    for k in turns:
        pieces = lax.psum_scatter(pieces, axes[k], scatter_dimension=0, tiled=True)
    return pieces[0]


def in_blocks(array, dim, devices):
    dims = array.shape
    pieces = array.reshape(*dims[:dim], devices, dims[dim] // devices, *dims[dim + 1 :])
    return jnp.moveaxis(pieces, dim, 0)


def summed_rows(array, axes, turns, dim):
    devices = lax.axis_size(axes)
    return sum_in_order(in_blocks(array, dim, devices), axes, turns)


def sent_and_summed(array, axis, dim):
    pieces = in_blocks(array, dim, lax.axis_size(axis))
    arrived = lax.all_to_all(pieces, axis, split_axis=0, concat_axis=0, tiled=True)
    return arrived.sum(axis=0)


def one_axis_at_a_time(array, axes):
    for axis in axes:
        array = lax.psum(array, axis)
    return array


def dot_first(left, right):
    return lax.dot_general(
        left,
        right,
        (((0,), (0,)), ((), ())),
        precision=lax.Precision.HIGHEST,
        preferred_element_type=jnp.float32,
    )


def dot_last(left, right):
    return lax.dot_general(
        left,
        right,
        (((1,), (1,)), ((), ())),
        precision=lax.Precision.HIGHEST,
        preferred_element_type=jnp.float32,
    )


def dot_plain(left, right):
    return jnp.dot(left, right, precision=lax.Precision.HIGHEST, preferred_element_type=jnp.float32)


def body(basis_out, basis_in, eig_damped, query_left, query_right, train_left, train_right):
    rank_width = query_right.shape[1]
    basis_rows = basis_out
    rot_left = dot_first(basis_rows, gathered_copies(query_left, COL, 0).astype(jnp.float32))
    rot_left = over_copies(rot_left, ROW)
    joined = jnp.concatenate([query_right, train_right], axis=1).astype(jnp.float32)
    share = summed_rows(dot_first(basis_in, joined), COL, (0, 2, 1), 0)
    piece = lax.all_gather(share, COL, axis=0, tiled=True)
    precond = dot_last(rot_left, piece[:, :rank_width]) / eig_damped
    contrib = dot_plain(precond, piece[:, rank_width:])
    applied = lax.psum(contrib, ROW)
    basis_rows = basis_out
    response = sent_and_summed(dot_plain(basis_rows, applied), COL, 0)
    partial_scores = jnp.sum(train_left.astype(jnp.float32) * response, axis=0)
    scores = one_axis_at_a_time(partial_scores, ROW_COL)
    return (response, scores)


def solution(mesh):
    finer = Mesh(mesh.devices.reshape(4, 2, 4, 2, 4), ("row_0", "row_1", "col_0", "col_1", "col_2"))
    placed = (
        P(ROW, COL),
        P(COL, ROW),
        P(COL, ROW),
        P(ROW_COL, None),
        P(COL, None),
        P(ROW_COL, None),
        P(COL, None),
    )
    return jax.shard_map(
        body, mesh=finer, in_specs=placed, out_specs=(P(ROW_COL, None), P()), check_vma=False
    )
```

profile of v0, /device:TPU:8, one launch (start us, length us, event | category | flops | bytes accessed | tf_op | source)
XLA Modules:
  0.0 579.2 jit_solution(16628478993421398997)
XLA Ops:
  7.2 9.0 %convolution_bitcast_fusion = f32[2048,768]{0,1:T(8,128)} fusion(f32[512,2048]{1,0:T(8,128)} %param.8, bf16[512,512]{1,0:T(8,128)(2,1)} %param.13, bf16[512,256]{1,0:T(8,128)(2,1)} %param.11), kind=kOutput, calls=%fused_computation.3 | convolution fusion | flops 9665249280 | bytes 11272192 | tf_op jit(solution)/shard_map/dot_general | solution.py:66
  16.2 6.6 %copy.12 = f32[2048,768]{1,0:T(8,128)} copy(f32[2048,768]{0,1:T(8,128)} %convolution_bitcast_fusion) | data formatting | bytes 12582912 | tf_op jit(solution)/shard_map/dot_general | solution.py:66
  22.8 6.1 %copy.13 = f32[4,4,2,64,768]{4,3,2,1,0:T(8,128)} copy(f32[4,4,2,64,768]{4,3,1,2,0:T(8,128)} %bitcast.18) | data formatting | bytes 12582912 | tf_op jit(solution)/shard_map/transpose | solution.py:35
  29.0 69.5 %reduce-scatter.4.cloned.1.call-done = f32[8,64,768]{2,1,0:T(8,128)} async-done(((f32[32,64,768]{2,1,0:T(8,128)}), f32[8,64,768]{2,1,0:T(8,128)}) %reduce-scatter.4.cloned.1.call-update) | async-done | bytes 1572880 | tf_op jit(solution)/shard_map/reduce_scatter | solution.py:38
  98.6 29.4 %reduce-scatter.6.cloned.1.call-done = f32[2,64,768]{2,1,0:T(8,128)} async-done(((f32[8,64,768]{2,1,0:T(8,128)}), f32[2,64,768]{2,1,0:T(8,128)}) %reduce-scatter.6.cloned.1.call-update) | async-done | bytes 393232 | tf_op jit(solution)/shard_map/reduce_scatter | solution.py:38
  128.0 21.8 %reduce-scatter.8.cloned.1.call-done = f32[1,64,768]{2,1,0:T(8,128)} async-done(((f32[2,64,768]{2,1,0:T(8,128)}), f32[1,64,768]{2,1,0:T(8,128)}) %reduce-scatter.8.cloned.1.call-update) | async-done | bytes 196624 | tf_op jit(solution)/shard_map/reduce_scatter | solution.py:38
  150.0 25.1 %all_to_all.15 = bf16[32,64,256]{2,1,0:T(8,128)(2,1)S(1)} all-to-all(bf16[32,64,256]{2,1,0:T(8,128)(2,1)S(1)} %broadcast_in_dim.6), channel_id=1, replica_groups=mesh['row_0'=4,'row_1'=2,'col_0'=4,'col_1'=2,'col_2'=4] {'col_0','col_1'..., dimensions={0} | all-to-all | bytes 2097152 | tf_op jit(solution)/shard_map/all_to_all | solution.py:20
  175.1 5.7 fusion.9
  180.8 0.4 broadcast_in_dim.7
  181.2 103.8 %all_to_all.16 = f32[8,512,256]{2,1,0:T(8,128)} all-to-all(f32[8,512,256]{2,1,0:T(8,128)S(1)} %broadcast_in_dim.7), channel_id=1, replica_groups=mesh['row_0'=4,'row_1'=2,'col_0'=4,'col_1'=2,'col_2'=4] {'row_0','row_1'}, dimensions={0} | all-to-all | bytes 8388608 | tf_op jit(solution)/shard_map/all_to_all | solution.py:20
  284.9 2.5 reduce_sum.27
  287.5 71.0 %all-gather.3.cloned.1.call-done = f32[1,2048,768]{2,1,0:T(8,128)} async-done(((f32[1,64,768]{2,1,0:T(8,128)}), f32[1,2048,768]{2,1,0:T(8,128)}) %all-gather.3.cloned.1.call-update) | async-done | bytes 6291472 | tf_op jit(solution)/shard_map/all_gather | solution.py:96
  358.4 5.6 fusion.3
  364.1 10.3 %fusion = f32[512,512]{1,0:T(8,128)} fusion(f32[2048,768]{1,0:T(8,128)S(1)} %bitcast.22, f32[512,2048]{1,0:T(8,128)S(1)} %fusion.3, f32[512,2048]{1,0:T(8,128)} %param.9), kind=kOutput, calls=%fused_computation | convolution fusion | flops 6443499520 | bytes 13631488 | tf_op jit(solution)/shard_map/dot_general | solution.py:86
  374.4 78.1 %all-reduce.2.cloned.1.call-done = f32[512,512]{1,0:T(8,128)} async-done(((f32[512,512]{1,0:T(8,128)}), f32[512,512]{1,0:T(8,128)}) %all-reduce.2.cloned.1.call-update) | async-done | bytes 1048592 | tf_op jit(solution)/shard_map/psum | solution.py:99
  452.6 16.6 %convolution_bitcast_fusion.1 = f32[2048,512]{0,1:T(8,128)} fusion(f32[512,512]{1,0:T(8,128)} %all-reduce.2.cloned.1.call-done, f32[2048,512]{1,0:T(8,128)} %param.7), kind=kOutput, calls=%fused_computation.4 | convolution fusion | flops 6442450944 | bytes 9437184 | tf_op jit(solution)/shard_map/dot_general | solution.py:86
  469.2 5.3 copy.14
  474.6 56.6 %all_to_all.17 = f32[32,64,512]{2,1,0:T(8,128)} all-to-all(f32[32,64,512]{2,1,0:T(8,128)} %bitcast.19), channel_id=1, replica_groups=mesh['row_0'=4,'row_1'=2,'col_0'=4,'col_1'=2,'col_2'=4] {'col_0','col_1'..., dimensions={0} | all-to-all | bytes 8388608 | tf_op jit(solution)/shard_map/all_to_all | solution.py:55
  531.2 2.6 reduce_sum.28
  533.8 10.9 %psum.43 = f32[512]{0:T(512)S(1)} all-reduce(f32[512]{0:T(512)S(1)} %multiply_reduce_fusion), channel_id=1, replica_groups=mesh['row_0'=4,'row_1'=2,'col_0'=4,'col_1'=2,'col_2'=4] {'row_0'}, use_global_device_ids=true, to_apply=%region_7.0 | all-reduce | flops 512 | bytes 4096 | tf_op jit(solution)/shard_map/psum | solution.py:61
  544.7 2.5 psum.44
  547.2 8.7 %psum.45 = f32[512]{0:T(512)S(1)} all-reduce(f32[512]{0:T(512)S(1)} %psum.44), channel_id=1, replica_groups=mesh['row_0'=4,'row_1'=2,'col_0'=4,'col_1'=2,'col_2'=4] {'col_0'}, use_global_device_ids=true, to_apply=%region_9.0 | all-reduce | flops 512 | bytes 4096 | tf_op jit(solution)/shard_map/psum | solution.py:61
  555.9 4.9 psum.46
  560.8 11.8 %psum.47 = f32[512]{0:T(512)} all-reduce(f32[512]{0:T(512)S(1)} %psum.46), channel_id=1, replica_groups=mesh['row_0'=4,'row_1'=2,'col_0'=4,'col_1'=2,'col_2'=4] {'col_2'}, use_global_device_ids=true, to_apply=%region_11.0 | all-reduce | flops 512 | bytes 4096 | tf_op jit(solution)/shard_map/psum | solution.py:61
  (20 shorter events, 0.4 us)
Async XLA Ops:
  7.2 91.3 %reduce-scatter.4.cloned.1.call-start = ((), (), s32[]{:S(2)}) async-start(), calls=%async_computation.6 | async-start | bytes 7864320 | tf_op jit(solution)/shard_map/reduce_scatter | solution.py:38
  28.9 120.9 %copy-start.3 = (bf16[64,256]{1,0:T(8,128)(2,1)S(1)}, bf16[64,256]{1,0:T(8,128)(2,1)}, u32[]{:S(2)}) copy-start(bf16[64,256]{1,0:T(8,128)(2,1)} %param.10) | copy-start | bytes 98308
  28.9 99.0 %reduce-scatter.6.cloned.1.call-start = ((), (), s32[]{:S(2)}) async-start(), calls=%async_computation.7 | async-start | bytes 1966080 | tf_op jit(solution)/shard_map/reduce_scatter | solution.py:38
  98.5 51.3 %reduce-scatter.8.cloned.1.call-start = ((), (), s32[]{:S(2)}) async-start(), calls=%async_computation.8 | async-start | bytes 589824 | tf_op jit(solution)/shard_map/reduce_scatter | solution.py:38
  127.9 230.5 %all-gather.3.cloned.1.call-start = ((), (), s32[]{:S(2)}) async-start(), calls=%async_computation.10 | async-start | bytes 6488064 | tf_op jit(solution)/shard_map/all_gather | solution.py:96
  149.8 302.8 %all-reduce.2.cloned.1.call-start = ((), (), s32[]{:S(2)}) async-start(), calls=%async_computation.9 | async-start | bytes 2097152 | tf_op jit(solution)/shard_map/psum | solution.py:99
  358.4 5.6 copy-start
  531.2 2.6 copy-start.2
  533.7 38.9 %copy-start.1 = (f32[64,512]{1,0:T(8,128)}, f32[64,512]{1,0:T(8,128)S(1)}, u32[]{:S(2)}) copy-start(f32[64,512]{1,0:T(8,128)S(1)} %reduce_sum.28) | copy-start | bytes 393220
Sparse Core Ops, SparseCore 0:
  29.1 69.3 reduce-scatter.3
  101.0 26.8 reduce-scatter.5
  130.4 19.3 reduce-scatter.7
  151.4 206.9 all-gather.2
  374.6 77.9 all-reduce.1
where the time goes:
time: 580 us; the launch traced here: 579 us
  waiting for transfers between devices  270 us (47%)
  blocking collectives  224 us (39%)
  matrix products  47.3 us (8%)
  local copies, waits for them, and re-layouts  18.6 us (3%)
  between operations  13.9 us (2%)
    all_to_all x2, blocking collectives, from_everyone(): return lax.all_to_all(copies, axis, split_axis=0, concat_axis=0, tiled=True)  129 us
    reduce_scatter x3, waiting for transfers between devices, sum_in_order(): pieces = lax.psum_scatter(pieces, axes[k], scatter_dimension=0, tiled=True)  121 us
    psum x1, waiting for transfers between devices, body(): applied = lax.psum(contrib, ROW)  78.1 us
    all_gather x1, waiting for transfers between devices, body(): piece = lax.all_gather(share, COL, axis=0, tiled=True)  71 us
    all_to_all x1, blocking collectives, sent_and_summed(): lax.all_to_all(pieces, axis, split_axis=0, concat_axis=0, tiled=True)  56.6 us
    psum x5, blocking collectives, one_axis_at_a_time(): array = lax.psum(array, axis)  38.9 us
    dot_general x2, matrix products, dot_plain(): jnp.dot(left, right, precision=lax.Precision.HIGHEST, preferred_element_t...  27 us
    dot_general x2, matrix products, dot_first(): lax.dot_general(left, right, (((0,), (0,)), ((), ())), precision=lax.Prec...  14.7 us
  transfers between devices with their start and end apart: 5, of which 5 were waited for; matrix products, arithmetic and copies ran while one was open for 2% of the time, Pallas kernels for 0%

commit v1 on v0

--- a/solution.py
+++ b/solution.py
@@ -93,7 +93,9 @@
     rot_left = over_copies(rot_left, ROW)
     joined = jnp.concatenate([query_right, train_right], axis=1).astype(jnp.float32)
     share = summed_rows(dot_first(basis_in, joined), COL, (0, 2, 1), 0)
-    piece = lax.all_gather(share, COL, axis=0, tiled=True)
+    piece = jnp.concatenate(
+        lax.all_to_all(jnp.stack([share] * lax.axis_size(COL)), COL, 0, 0), axis=0
+    )
     precond = dot_last(rot_left, piece[:, :rank_width]) / eig_damped
     contrib = dot_plain(precond, piece[:, rank_width:])
     applied = lax.psum(contrib, ROW)

time: 580 us -> 502 us (0.87)
  blocking collectives: 224 us -> 123 us
  starting transfers between devices: 0.19 us -> 17 us
  local copies, waits for them, and re-layouts: 18.6 us -> 25.5 us
    all_to_all x0 -> x2, waiting for transfers between devices: none -> 126 us  [the longest x1 90.6 us: body(): lax.all_to_all(jnp.stack([share] * lax.axis_size(COL)), COL, 0, 0)]
    all_to_all x2 -> x1, blocking collectives: 129 us -> 27.2 us  [from_everyone(): return lax.all_to_all(copies, axis, split_axis=0, concat_axis=0, tiled=True)]
    all_gather x1 -> x0, waiting for transfers between devices: 71 us -> none  [body(): piece = lax.all_gather(share, COL, axis=0, tiled=True)]
    reduce_scatter x3, waiting for transfers between devices: 121 us -> 63.3 us  [sum_in_order(): pieces = lax.psum_scatter(pieces, axes[k], scatter_dimension=0, tiled=True)]
    all_to_all x0 -> x2, starting transfers between devices: none -> 16.6 us  [the longest x1 8.8 us: body(): lax.all_to_all(jnp.stack([share] * lax.axis_size(COL)), COL, 0, 0)]
  transfers between devices with their start and end apart: 5 -> 6, of which waited for: 5 -> 6; matrix products, arithmetic and copies ran while one was open for 2% -> 2% of each run, Pallas kernels for 0% -> 0%
where the time goes in v1:
time: 502 us
  waiting for transfers between devices  271 us (54%)
  blocking collectives  123 us (25%)
  matrix products  46.7 us (9%)
  local copies, waits for them, and re-layouts  25.5 us (5%)
  starting transfers between devices  17 us (3%)
  between operations  13.8 us (3%)
  other arithmetic  5.12 us (1%)
    all_to_all x1, waiting for transfers between devices, body(): lax.all_to_all(jnp.stack([share] * lax.axis_size(COL)), COL, 0, 0)  90.6 us
    psum x1, waiting for transfers between devices, body(): applied = lax.psum(contrib, ROW)  81.9 us
    reduce_scatter x3, waiting for transfers between devices, sum_in_order(): pieces = lax.psum_scatter(pieces, axes[k], scatter_dimension=0, tiled=True)  63.3 us
    all_to_all x1, blocking collectives, sent_and_summed(): lax.all_to_all(pieces, axis, split_axis=0, concat_axis=0, tiled=True)  56.6 us
    psum x5, blocking collectives, one_axis_at_a_time(): array = lax.psum(array, axis)  38.9 us
    all_to_all x1, waiting for transfers between devices, from_everyone(): return lax.all_to_all(copies, axis, split_axis=0, concat_axis=0, tiled=True)  35 us
    all_to_all x1, blocking collectives, from_everyone(): return lax.all_to_all(copies, axis, split_axis=0, concat_axis=0, tiled=True)  27.2 us
    dot_general x2, matrix products, dot_plain(): jnp.dot(left, right, precision=lax.Precision.HIGHEST, preferred_element_t...  26.4 us
  transfers between devices with their start and end apart: 6, of which 6 were waited for; matrix products, arithmetic and copies ran while one was open for 2% of the time, Pallas kernels for 0%

profile of v1, /device:TPU:8, one launch (start us, length us, event | category | flops | bytes accessed | tf_op | source)
XLA Modules:
  0.0 501.6 jit_solution(13159863466746664863)
XLA Ops:
  7.2 8.9 %convolution_bitcast_fusion = f32[2048,768]{0,1:T(8,128)} fusion(f32[512,2048]{1,0:T(8,128)} %param.8, bf16[512,512]{1,0:T(8,128)(2,1)} %param.13, bf16[512,256]{1,0:T(8,128)(2,1)} %param.11), kind=kOutput, calls=%fused_computation.3 | convolution fusion | flops 9665249280 | bytes 11272192 | tf_op jit(solution)/shard_map/dot_general | solution.py:66
  16.1 6.5 %copy.12 = f32[2048,768]{1,0:T(8,128)} copy(f32[2048,768]{0,1:T(8,128)} %convolution_bitcast_fusion) | data formatting | bytes 12582912 | tf_op jit(solution)/shard_map/dot_general | solution.py:66
  22.6 6.1 %copy.13 = f32[4,4,2,64,768]{4,3,2,1,0:T(8,128)} copy(f32[4,4,2,64,768]{4,3,1,2,0:T(8,128)} %bitcast.19) | data formatting | bytes 12582912 | tf_op jit(solution)/shard_map/transpose | solution.py:35
  29.6 27.2 %all_to_all.20 = bf16[32,64,256]{2,1,0:T(8,128)(2,1)S(1)} all-to-all(bf16[32,64,256]{2,1,0:T(8,128)(2,1)S(1)} %broadcast_in_dim.6), channel_id=1, replica_groups=mesh['row_0'=4,'row_1'=2,'col_0'=4,'col_1'=2,'col_2'=4] {'col_0','col_1'..., dimensions={0} | all-to-all | bytes 2097152 | tf_op jit(solution)/shard_map/all_to_all | solution.py:20
  56.8 5.8 %fusion.9 = f32[512,256]{1,0:T(8,128)S(1)} fusion(f32[2048,512]{1,0:T(8,128)} %param.7, bf16[2048,256]{1,0:T(8,128)(2,1)S(1)} %bitcast.21), kind=kOutput, calls=%fused_computation.12 | convolution fusion | flops 3221225472 | bytes 5767168 | tf_op jit(solution)/shard_map/dot_general | solution.py:66
  65.0 7.8 %all-to-all-start.1 = ((f32[8,512,256]{2,1,0:T(8,128)}), f32[8,512,256]{2,1,0:T(8,128)}, u32[]{:S(2)}, u32[]{:S(2)}) async-start(f32[8,512,256]{2,1,0:T(8,128)} %broadcast_in_dim.7), calls=%async_computation.1 | async-start | bytes 8388608 | tf_op jit(solution)/shard_map/all_to_all | solution.py:20
  72.9 31.8 %reduce-scatter.4.cloned.1.call-done = f32[8,64,768]{2,1,0:T(8,128)} async-done(((f32[32,64,768]{2,1,0:T(8,128)}), f32[8,64,768]{2,1,0:T(8,128)}) %reduce-scatter.4.cloned.1.call-update) | async-done | bytes 1572880 | tf_op jit(solution)/shard_map/reduce_scatter | solution.py:38
  104.8 29.9 %reduce-scatter.6.cloned.1.call-done = f32[2,64,768]{2,1,0:T(8,128)} async-done(((f32[8,64,768]{2,1,0:T(8,128)}), f32[2,64,768]{2,1,0:T(8,128)}) %reduce-scatter.6.cloned.1.call-update) | async-done | bytes 393232 | tf_op jit(solution)/shard_map/reduce_scatter | solution.py:38
  134.7 35.0 %all-to-all-done.1 = f32[8,512,256]{2,1,0:T(8,128)} async-done(((f32[8,512,256]{2,1,0:T(8,128)}), f32[8,512,256]{2,1,0:T(8,128)}, u32[]{:S(2)}, u32[]{:S(2)}) %all-to-all-start.1) | async-done | bytes 4194336 | tf_op jit(solution)/shard_map/all_to_all | solution.py:20
  171.3 4.3 stack.3
  175.6 8.8 %all-to-all-start.2 = ((f32[32,64,768]{2,1,0:T(8,128)}), f32[32,64,768]{2,1,0:T(8,128)}, u32[]{:S(2)}, u32[]{:S(2)}) async-start(f32[32,64,768]{2,1,0:T(8,128)} %stack.3), calls=%async_computation.5 | async-start | bytes 12582912 | tf_op jit(solution)/shard_map/all_to_all | solution.py:97
  184.6 2.5 reduce_sum.27
  187.1 90.6 %all-to-all-done.2 = f32[32,64,768]{2,1,0:T(8,128)} async-done(((f32[32,64,768]{2,1,0:T(8,128)}), f32[32,64,768]{2,1,0:T(8,128)}, u32[]{:S(2)}, u32[]{:S(2)}) %all-to-all-start.2) | async-done | bytes 6291488 | tf_op jit(solution)/shard_map/all_to_all | solution.py:97
  277.7 5.6 %fusion.3 = f32[512,2048]{1,0:T(8,128)S(1)} fusion(f32[512,256]{1,0:T(8,128)S(1)} %reduce_sum.27, f32[2048,768]{1,0:T(8,128)} %bitcast.6), kind=kOutput, calls=%fused_computation.5 | convolution fusion | flops 3221225472 | bytes 6815744 | tf_op jit(solution)/shard_map/dot_general | solution.py:76
  283.4 9.7 %fusion = f32[512,512]{1,0:T(8,128)} fusion(f32[2048,768]{1,0:T(8,128)} %bitcast.6, f32[512,2048]{1,0:T(8,128)S(1)} %fusion.3, f32[512,2048]{1,0:T(8,128)S(1)} %copy-done.3), kind=kOutput, calls=%fused_computation | convolution fusion | flops 6443499520 | bytes 13631488 | tf_op jit(solution)/shard_map/dot_general | solution.py:86
  293.1 81.9 %all-reduce.2.cloned.1.call-done = f32[512,512]{1,0:T(8,128)} async-done(((f32[512,512]{1,0:T(8,128)}), f32[512,512]{1,0:T(8,128)}) %all-reduce.2.cloned.1.call-update) | async-done | bytes 1048592 | tf_op jit(solution)/shard_map/psum | solution.py:101
  375.0 16.6 %convolution_bitcast_fusion.1 = f32[2048,512]{0,1:T(8,128)} fusion(f32[512,512]{1,0:T(8,128)} %all-reduce.2.cloned.1.call-done, f32[2048,512]{1,0:T(8,128)} %param.7), kind=kOutput, calls=%fused_computation.4 | convolution fusion | flops 6442450944 | bytes 9437184 | tf_op jit(solution)/shard_map/dot_general | solution.py:86
  391.6 5.3 %copy.14 = f32[2048,512]{1,0:T(8,128)} copy(f32[2048,512]{0,1:T(8,128)} %convolution_bitcast_fusion.1) | data formatting | bytes 8388608 | tf_op jit(solution)/shard_map/dot_general | solution.py:86
  397.0 56.6 %all_to_all.21 = f32[32,64,512]{2,1,0:T(8,128)} all-to-all(f32[32,64,512]{2,1,0:T(8,128)} %bitcast.20), channel_id=1, replica_groups=mesh['row_0'=4,'row_1'=2,'col_0'=4,'col_1'=2,'col_2'=4] {'col_0','col_1'..., dimensions={0} | all-to-all | bytes 8388608 | tf_op jit(solution)/shard_map/all_to_all | solution.py:55
  453.6 2.6 reduce_sum.28
  456.2 10.9 %psum.43 = f32[512]{0:T(512)S(1)} all-reduce(f32[512]{0:T(512)S(1)} %multiply_reduce_fusion), channel_id=1, replica_groups=mesh['row_0'=4,'row_1'=2,'col_0'=4,'col_1'=2,'col_2'=4] {'row_0'}, use_global_device_ids=true, to_apply=%region_7.0 | all-reduce | flops 512 | bytes 4096 | tf_op jit(solution)/shard_map/psum | solution.py:61
  469.6 8.7 %psum.45 = f32[512]{0:T(512)S(1)} all-reduce(f32[512]{0:T(512)S(1)} %psum.44), channel_id=1, replica_groups=mesh['row_0'=4,'row_1'=2,'col_0'=4,'col_1'=2,'col_2'=4] {'col_0'}, use_global_device_ids=true, to_apply=%region_9.0 | all-reduce | flops 512 | bytes 4096 | tf_op jit(solution)/shard_map/psum | solution.py:61
  478.3 4.9 psum.46
  483.2 11.8 %psum.47 = f32[512]{0:T(512)} all-reduce(f32[512]{0:T(512)S(1)} %psum.46), channel_id=1, replica_groups=mesh['row_0'=4,'row_1'=2,'col_0'=4,'col_1'=2,'col_2'=4] {'col_2'}, use_global_device_ids=true, to_apply=%region_11.0 | all-reduce | flops 512 | bytes 4096 | tf_op jit(solution)/shard_map/psum | solution.py:61
  (21 shorter events, 7.7 us)
Async XLA Ops:
  7.2 97.6 %reduce-scatter.4.cloned.1.call-start = ((), (), s32[]{:S(2)}) async-start(), calls=%async_computation.7 | async-start | bytes 7864320 | tf_op jit(solution)/shard_map/reduce_scatter | solution.py:38
  28.7 0.8 copy-start.2
  65.0 104.7 %all-to-all-start.1 = ((f32[8,512,256]{2,1,0:T(8,128)}), f32[8,512,256]{2,1,0:T(8,128)}, u32[]{:S(2)}, u32[]{:S(2)}) async-start(f32[8,512,256]{2,1,0:T(8,128)} %broadcast_in_dim.7), calls=%async_computation.1 | async-start | bytes 8388608 | tf_op jit(solution)/shard_map/all_to_all | solution.py:20
  72.9 61.8 %reduce-scatter.6.cloned.1.call-start = ((), (), s32[]{:S(2)}) async-start(), calls=%async_computation.8 | async-start | bytes 1966080 | tf_op jit(solution)/shard_map/reduce_scatter | solution.py:38
  104.8 66.5 %reduce-scatter.8.cloned.1.call-start = ((), (), s32[]{:S(2)}) async-start(), calls=%async_computation.9 | async-start | bytes 589824 | tf_op jit(solution)/shard_map/reduce_scatter | solution.py:38
  175.6 102.2 %all-to-all-start.2 = ((f32[32,64,768]{2,1,0:T(8,128)}), f32[32,64,768]{2,1,0:T(8,128)}, u32[]{:S(2)}, u32[]{:S(2)}) async-start(f32[32,64,768]{2,1,0:T(8,128)} %stack.3), calls=%async_computation.5 | async-start | bytes 12582912 | tf_op jit(solution)/shard_map/all_to_all | solution.py:97
  184.4 190.6 %all-reduce.2.cloned.1.call-start = ((), (), s32[]{:S(2)}) async-start(), calls=%async_computation.10 | async-start | bytes 2097152 | tf_op jit(solution)/shard_map/psum | solution.py:101
  277.7 5.6 %copy-start.3 = (f32[512,2048]{1,0:T(8,128)S(1)}, f32[512,2048]{1,0:T(8,128)}, u32[]{:S(2)}) copy-start(f32[512,2048]{1,0:T(8,128)} %param.9) | copy-start | bytes 12582916
  453.6 2.6 copy-start.1
  456.2 38.9 %copy-start = (f32[64,512]{1,0:T(8,128)}, f32[64,512]{1,0:T(8,128)S(1)}, u32[]{:S(2)}) copy-start(f32[64,512]{1,0:T(8,128)S(1)} %reduce_sum.28) | copy-start | bytes 393220
Sparse Core Ops, SparseCore 0:
  28.9 75.8 reduce-scatter.3
  107.3 27.3 reduce-scatter.5
  137.2 34.0 reduce-scatter.7
  293.2 81.6 all-reduce.1
